TPU v7x, 32 devices: a whole 2x2x4 slice. The times are simulated.
32 devices in a mesh: dp: 4 (over y, x), inner: 8 (over z, core).
Axes of the slice: x: 2, y: 2, z: 4, core: 2. Of those that a mesh axis runs over, the one named last changes fastest.
Arguments:
- queries: bfloat16 [32, 32, 128], P(('dp', 'inner'))
- labels: int32 [32], P(('dp', 'inner')), may hold values from 0 to 127
- pages: bfloat16 [128, 1024, 128], P(('dp', 'inner'))
Outputs:
- grad_queries: float32 [32, 32, 128], P(('dp', 'inner'))
- grad_pages: float32 [128, 1024, 128], P(('dp', 'inner'))
All inputs are finite; a program needn't handle non-finite values.
Results may differ from a plain program's by a relative error of at most 0.0029.
Values may be sent and summed in bfloat16 or wider, within the bound.
No kernel may reach another device: no remote copies, remote signals or barrier semaphores. Data moves between devices by JAX's collectives and lax.ppermute only.
A program may use at most 64 MiB of HBM per device.

v0:
```python
import jax
import jax.numpy as jnp
from jax import lax
from jax.sharding import PartitionSpec as P


def shards(queries, labels, pages):
    pages_here, patch_count, width = pages.shape
    token_count = queries.shape[1]
    first_page = lax.axis_index(("dp", "inner")) * pages_here

    def block_terms(query_block, label_block, page_grads):
        rows_count = query_block.shape[0]
        flat_rows = query_block.reshape(rows_count * token_count, width)
        query_grad = jnp.zeros((rows_count * token_count, width), jnp.float32)
        updated = []
        for page_slot in range(pages_here):
            page_block = pages[page_slot]
            scores = lax.dot_general(
                flat_rows, page_block, (((1,), (1,)), ((), ())), preferred_element_type=jnp.float32
            )
            weights = jax.nn.softmax(scores, axis=-1)
            matched = jnp.sum(weights * scores, axis=-1)
            summed = matched.reshape(rows_count, token_count).sum(axis=1)
            signs = jnp.where(
                label_block == first_page + page_slot, jnp.float32(1.0), jnp.float32(-1.0)
            )
            logits = summed - jnp.float32(token_count)
            grad_score = -signs * jax.nn.sigmoid(-signs * logits)
            row_grad = jnp.broadcast_to(grad_score[:, None], (rows_count, token_count)).reshape(
                rows_count * token_count
            )
            dscore = (row_grad[:, None] * weights * (1.0 + scores - matched[:, None])).astype(
                jnp.bfloat16
            )
            query_grad = query_grad + jnp.dot(
                dscore, page_block, preferred_element_type=jnp.float32
            )
            page_term = lax.dot_general(
                dscore, flat_rows, (((0,), (0,)), ((), ())), preferred_element_type=jnp.float32
            )
            updated.append(page_grads[page_slot] + page_term)
        return (query_grad.reshape(rows_count, token_count, width), jnp.stack(updated))

    empty_pages = jnp.zeros((pages_here, patch_count, width), jnp.float32)
    every_query, every_label = (
        lax.all_gather(queries, ("dp", "inner"), axis=0, tiled=True),
        lax.all_gather(labels, ("dp", "inner"), axis=0, tiled=True),
    )
    page_grads = empty_pages
    rows_count = every_query.shape[0]
    query_blocks = every_query.reshape(rows_count // 16, 16, token_count, width)
    label_blocks = every_label.reshape(rows_count // 16, 16)

    def advance(page_carry, inputs):
        block_grad, page_carry = block_terms(inputs[0], inputs[1], page_carry)
        return (page_carry, block_grad)

    page_grads, block_grads = lax.scan(advance, page_grads, (query_blocks, label_blocks))
    grad_buffer = block_grads.reshape(rows_count, token_count, width)
    partial_sum = lax.psum_scatter(
        grad_buffer.astype(jnp.bfloat16), "dp", scatter_dimension=0, tiled=True
    ).astype(jnp.float32)
    grad_queries = lax.psum_scatter(partial_sum, "inner", scatter_dimension=0, tiled=True)
    return (grad_queries, page_grads)


def solution(mesh):
    placed = (P(("dp", "inner"), None, None), P(("dp", "inner")), P(("dp", "inner"), None, None))
    return jax.shard_map(
        shards,
        mesh=mesh,
        in_specs=placed,
        out_specs=(P(("dp", "inner"), None, None), P(("dp", "inner"), None, None)),
        check_vma=False,
    )
```

profile of v0, /device:TPU:0, one launch (start us, length us, event | category | flops | bytes accessed | tf_op | source)
XLA Modules:
  0.0 223.1 jit_solution(10414008605873370452)
XLA Ops:
  8.1 42.0 %all-reduce = s32[32]{0:T(128)S(1)} all-reduce(s32[32]{0:T(128)S(1)} %dynamic-update-slice), channel_id=1, replica_groups=mesh['dp'=4,'inner'=8] {'dp','inner'}, use_global_device_ids=true, to_apply=%add | all-reduce | flops 32 | bytes 256
  50.1 41.4 %all_gather.7 = bf16[32,32,128]{2,1,0:T(8,128)(2,1)S(1)} all-gather(bf16[1,32,128]{2,1,0:T(8,128)(2,1)} %param.5), channel_id=1, replica_groups=mesh['dp'=4,'inner'=8] {'dp','inner'}, dimensions={0}, use_global_device_ids=true | all-gather | bytes 270336 | tf_op jit(solution)/shard_map/all_gather | solution.py:47
  91.6 1.5 broadcast_in_dim.86
  93.0 68.0 %while.15 = (s32[]{:T(128)}, f32[4,1024,128]{2,1,0:T(8,128)}, bf16[2,16,32,128]{3,2,1,0:T(8,128)(2,1)}, s32[2,16]{1,0:T(2,128)S(1)}, s32[]{:T(128)}, /*index=5*/...) while((s32[]{:T(128)}, f32[4,1024,128]{2,1,0:T(8,128)}, ...), condition=%wide.region_17.18_spmd, body=%wide.region_0.17_spmd.sunk | while | flops 1642328576 | bytes 108293800 | solution.py:59
  94.1 0.8 copy-done
  99.6 0.8 copy-done.2
  101.9 2.3 %multiply_convert_fusion.11 = bf16[512,1024]{1,0:T(8,128)(2,1)S(1)} fusion(f32[512,1024]{1,0:T(8,128)} %copy-done.2, f32[512]{0:T(512)S(1)} %multiply_reduce_fusion.9, f32[512]{0:T(512)S(1)} %mul.311, f32[512]{0:T(512)S(1)} %fusion.117, f32[512]{0:T(512)S(1)} %get-tuple-element.248), kind=kLoop, calls=%fused_computation.10.clone.1 | loop fusion | flops 3670016 | bytes 3153920 | tf_op jit(solution)/shard_map/while/body/eval_jaxpr/convert_element_type | solution.py:33
  104.6 2.3 %fusion.125 = f32[1,1024,128]{2,1,0:T(8,128)} fusion(bf16[512,1024]{1,0:T(8,128)(2,1)S(1)} %multiply_convert_fusion.11, bf16[512,128]{1,0:T(8,128)(2,1)S(1)} %bitcast.155, f32[4,1024,128]{2,1,0:T(8,128)} %get-tuple-element.271), kind=kOutput, calls=%fused_computation.25.clone.1 | convolution fusion | flops 134348800 | bytes 2228224 | tf_op jit(solution)/shard_map/while/body/eval_jaxpr/dot_general | solution.py:39
  108.0 0.8 copy-done.1
  110.3 3.2 %multiply_convert_fusion.8 = bf16[512,1024]{1,0:T(8,128)(2,1)} fusion(f32[512,1024]{1,0:T(8,128)} %copy-done.1, f32[512]{0:T(512)S(1)} %multiply_reduce_fusion.8, f32[512]{0:T(512)S(1)} %mul.308, f32[512]{0:T(512)S(1)} %fusion.115, f32[512]{0:T(512)S(1)} %get-tuple-element.246), kind=kLoop, calls=%fused_computation.1.clone.1 | loop fusion | flops 3670016 | bytes 3153920 | tf_op jit(solution)/shard_map/while/body/eval_jaxpr/convert_element_type | solution.py:33
  113.7 2.3 %multiply_convert_fusion.9 = bf16[512,1024]{1,0:T(8,128)(2,1)S(1)} fusion(f32[512,1024]{1,0:T(8,128)} %copy-done, f32[512]{0:T(512)} %copy-done.10, f32[512]{0:T(512)S(1)} %mul.309, f32[512]{0:T(512)} %copy-done.12, f32[512]{0:T(512)S(1)} %get-tuple-element.253), kind=kLoop, calls=%fused_computation.4.clone.1 | loop fusion | flops 3670016 | bytes 3153920 | tf_op jit(solution)/shard_map/while/body/eval_jaxpr/convert_element_type | solution.py:33
  117.3 1.5 multiply_convert_fusion.10
  118.8 1.4 convolution_add_fusion.10
  120.7 1.5 convolution_add_fusion.11
  122.7 1.4 convolution_add_fusion.12
  124.7 1.6 pad_maximum_fusion.2
  126.3 0.7 copy-done.14
  128.1 0.8 copy-done
  133.6 0.8 copy-done.2
  135.9 2.3 %multiply_convert_fusion.11 = bf16[512,1024]{1,0:T(8,128)(2,1)S(1)} fusion(f32[512,1024]{1,0:T(8,128)} %copy-done.2, f32[512]{0:T(512)S(1)} %multiply_reduce_fusion.9, f32[512]{0:T(512)S(1)} %mul.311, f32[512]{0:T(512)S(1)} %fusion.117, f32[512]{0:T(512)S(1)} %get-tuple-element.248), kind=kLoop, calls=%fused_computation.10.clone.1 | loop fusion | flops 3670016 | bytes 3153920 | tf_op jit(solution)/shard_map/while/body/eval_jaxpr/convert_element_type | solution.py:33
  138.6 2.3 %fusion.125 = f32[1,1024,128]{2,1,0:T(8,128)} fusion(bf16[512,1024]{1,0:T(8,128)(2,1)S(1)} %multiply_convert_fusion.11, bf16[512,128]{1,0:T(8,128)(2,1)S(1)} %bitcast.155, f32[4,1024,128]{2,1,0:T(8,128)} %get-tuple-element.271), kind=kOutput, calls=%fused_computation.25.clone.1 | convolution fusion | flops 134348800 | bytes 2228224 | tf_op jit(solution)/shard_map/while/body/eval_jaxpr/dot_general | solution.py:39
  142.0 0.8 copy-done.1
  144.3 3.2 %multiply_convert_fusion.8 = bf16[512,1024]{1,0:T(8,128)(2,1)} fusion(f32[512,1024]{1,0:T(8,128)} %copy-done.1, f32[512]{0:T(512)S(1)} %multiply_reduce_fusion.8, f32[512]{0:T(512)S(1)} %mul.308, f32[512]{0:T(512)S(1)} %fusion.115, f32[512]{0:T(512)S(1)} %get-tuple-element.246), kind=kLoop, calls=%fused_computation.1.clone.1 | loop fusion | flops 3670016 | bytes 3153920 | tf_op jit(solution)/shard_map/while/body/eval_jaxpr/convert_element_type | solution.py:33
  147.7 2.3 %multiply_convert_fusion.9 = bf16[512,1024]{1,0:T(8,128)(2,1)S(1)} fusion(f32[512,1024]{1,0:T(8,128)} %copy-done, f32[512]{0:T(512)} %copy-done.10, f32[512]{0:T(512)S(1)} %mul.309, f32[512]{0:T(512)} %copy-done.12, f32[512]{0:T(512)S(1)} %get-tuple-element.253), kind=kLoop, calls=%fused_computation.4.clone.1 | loop fusion | flops 3670016 | bytes 3153920 | tf_op jit(solution)/shard_map/while/body/eval_jaxpr/convert_element_type | solution.py:33
  151.3 1.5 multiply_convert_fusion.10
  152.8 1.4 convolution_add_fusion.10
  154.7 1.5 convolution_add_fusion.11
  156.7 1.4 convolution_add_fusion.12
  158.7 1.6 pad_maximum_fusion.2
  161.1 21.7 %reduce-scatter.3.cloned.1.call-done = bf16[8,32,128]{2,1,0:T(8,128)(2,1)} async-done(((bf16[32,32,128]{2,1,0:T(8,128)(2,1)}), bf16[8,32,128]{2,1,0:T(8,128)(2,1)}) %reduce-scatter.3.cloned.1.call-update) | async-done | bytes 65552 | tf_op jit(solution)/shard_map/reduce_scatter | solution.py:61
  182.8 1.5 convert_element_type.39
  184.3 31.9 %reduce-scatter.5.cloned.1.call-done = f32[1,32,128]{2,1,0:T(8,128)} async-done(((f32[8,32,128]{2,1,0:T(8,128)}), f32[1,32,128]{2,1,0:T(8,128)}) %reduce-scatter.5.cloned.1.call-update) | async-done | bytes 16400 | tf_op jit(solution)/shard_map/reduce_scatter | solution.py:64
  (151 shorter events, 27.4 us)
Async XLA Ops:
  7.2 85.8 %copy-start.4 = (bf16[4,1024,128]{2,1,0:T(8,128)(2,1)S(1)}, bf16[4,1024,128]{2,1,0:T(8,128)(2,1)}, u32[]{:S(2)}) copy-start(bf16[4,1024,128]{2,1,0:T(8,128)(2,1)} %param.7) | copy-start | bytes 3145732
  7.2 175.6 %reduce-scatter.3.cloned.1.call-start = ((), (), s32[]{:S(2)}) async-start(), calls=%async_computation.2 | async-start | bytes 327680 | tf_op jit(solution)/shard_map/reduce_scatter | solution.py:61
  93.0 8.2 %copy-start.18 = (s32[2,16]{1,0:T(2,128)}, s32[2,16]{1,0:T(2,128)S(1)}, u32[]{:S(2)}) copy-start(s32[2,16]{1,0:T(2,128)S(1)} %get-tuple-element.285) | copy-start | bytes 388 | tf_op jit(solution)/shard_map/while
  93.5 1.4 copy-start
  94.9 1.8 copy-start.12
  95.5 1.7 copy-start.10
  99.1 1.3 copy-start.2
  107.5 2.1 copy-start.15
  107.5 2.1 copy-start.16
  107.5 2.1 copy-start.17
  117.3 2.9 %copy-start.6 = (f32[4,1024,128]{2,1,0:T(8,128)S(1)}, f32[4,1024,128]{2,1,0:T(8,128)}, u32[]{:S(2)}) copy-start(f32[4,1024,128]{2,1,0:T(8,128)} %get-tuple-element.271) | copy-start | bytes 6291460 | tf_op jit(solution)/shard_map/while
  120.7 2.0 copy-start.3
  122.7 1.9 copy-start.7
  124.6 1.6 copy-start.13
  124.7 2.3 %copy-start.5 = (bf16[4,1024,128]{2,1,0:T(8,128)(2,1)S(1)}, bf16[4,1024,128]{2,1,0:T(8,128)(2,1)}, u32[]{:S(2)}) copy-start(bf16[4,1024,128]{2,1,0:T(8,128)(2,1)} %get-tuple-element.308) | copy-start | bytes 3145732 | tf_op jit(solution)/shard_map/while
  124.7 2.3 %copy-start.9 = (bf16[2,16,32,128]{3,2,1,0:T(8,128)(2,1)S(1)}, bf16[2,16,32,128]{3,2,1,0:T(8,128)(2,1)}, u32[]{:S(2)}) copy-start(bf16[2,16,32,128]{3,2,1,0:T(8,128)(2,1)} %copy-done.8) | copy-start | bytes 786436 | tf_op jit(solution)/shard_map/while
  124.7 2.3 %copy-start.19 = (s32[2,16]{1,0:T(2,128)S(1)}, s32[2,16]{1,0:T(2,128)}, u32[]{:S(2)}) copy-start(s32[2,16]{1,0:T(2,128)} %copy-done.18) | copy-start | bytes 388 | tf_op jit(solution)/shard_map/while
  127.0 8.2 %copy-start.18 = (s32[2,16]{1,0:T(2,128)}, s32[2,16]{1,0:T(2,128)S(1)}, u32[]{:S(2)}) copy-start(s32[2,16]{1,0:T(2,128)S(1)} %get-tuple-element.285) | copy-start | bytes 388 | tf_op jit(solution)/shard_map/while
  127.5 1.4 copy-start
  128.9 1.8 copy-start.12
  129.5 1.7 copy-start.10
  141.5 2.1 copy-start.15
  141.5 2.1 copy-start.16
  141.5 2.1 copy-start.17
  151.3 2.9 %copy-start.6 = (f32[4,1024,128]{2,1,0:T(8,128)S(1)}, f32[4,1024,128]{2,1,0:T(8,128)}, u32[]{:S(2)}) copy-start(f32[4,1024,128]{2,1,0:T(8,128)} %get-tuple-element.271) | copy-start | bytes 6291460 | tf_op jit(solution)/shard_map/while
  154.7 2.0 copy-start.3
  156.7 1.9 copy-start.7
  158.6 1.6 copy-start.13
  158.7 2.3 %copy-start.5 = (bf16[4,1024,128]{2,1,0:T(8,128)(2,1)S(1)}, bf16[4,1024,128]{2,1,0:T(8,128)(2,1)}, u32[]{:S(2)}) copy-start(bf16[4,1024,128]{2,1,0:T(8,128)(2,1)} %get-tuple-element.308) | copy-start | bytes 3145732 | tf_op jit(solution)/shard_map/while
  158.7 2.3 %copy-start.9 = (bf16[2,16,32,128]{3,2,1,0:T(8,128)(2,1)S(1)}, bf16[2,16,32,128]{3,2,1,0:T(8,128)(2,1)}, u32[]{:S(2)}) copy-start(bf16[2,16,32,128]{3,2,1,0:T(8,128)(2,1)} %copy-done.8) | copy-start | bytes 786436 | tf_op jit(solution)/shard_map/while
  158.7 2.3 %copy-start.19 = (s32[2,16]{1,0:T(2,128)S(1)}, s32[2,16]{1,0:T(2,128)}, u32[]{:S(2)}) copy-start(s32[2,16]{1,0:T(2,128)} %copy-done.18) | copy-start | bytes 388 | tf_op jit(solution)/shard_map/while
  161.0 55.2 %reduce-scatter.5.cloned.1.call-start = ((), (), s32[]{:S(2)}) async-start(), calls=%async_computation.3 | async-start | bytes 147456 | tf_op jit(solution)/shard_map/reduce_scatter | solution.py:64
  (9 other events, 8.8 us)
Sparse Core Ops, SparseCore 0:
  161.1 21.6 reduce-scatter.2
  185.6 30.5 reduce-scatter.4
where the time goes:
time: 224 us; the launch traced here: 223 us
  blocking collectives  83.4 us (37%)
  waiting for transfers between devices  53.7 us (24%)
  other arithmetic  37.3 us (17%)
  matrix products  21.1 us (9%)
  between operations  14.8 us (7%)
  local copies, waits for them, and re-layouts  12.2 us (5%)
    unnamed x1, blocking collectives  42 us
    all_gather x1, blocking collectives, shards(): lax.all_gather(queries, ('dp', 'inner'), axis=0, tiled=True)  41.4 us
    reduce_scatter x1, waiting for transfers between devices, shards(): lax.psum_scatter(partial_sum, 'inner', scatter_dimension=0, tiled=True)  31.9 us
    reduce_scatter x1, waiting for transfers between devices, shards(): lax.psum_scatter(grad_buffer.astype(jnp.bfloat16), 'dp', scatter_dimensio...  21.7 us
    convert_element_type x8, other arithmetic, block_terms(): (row_grad[:, None] * weights * (1.0 + scores - matched[:, None])).astype(...  18.5 us
    dot_general x8, matrix products, block_terms(): jnp.dot(dscore, page_block, preferred_element_type=jnp.float32)  9.52 us
    dot_general x8, matrix products, block_terms(): lax.dot_general(dscore, flat_rows, (((0,), (0,)), ((), ())), preferred_el...  7.48 us
    while x76, local copies, waits for them, and re-layouts  6.3 us
  transfers between devices with their start and end apart: 2, of which 2 were waited for; matrix products, arithmetic and copies ran while one was open for 0% of the time, Pallas kernels for 0%

commit v1 on v0

--- a/solution.py
+++ b/solution.py
@@ -2,6 +2,18 @@
 import jax.numpy as jnp
 from jax import lax
 from jax.sharding import PartitionSpec as P
+
+
+def gather_by_bits(x, axis, dim):
+    ways, here, step = (lax.axis_size(axis), lax.axis_index(axis), x.shape[dim])
+    line, have = (x, 1)
+    while have < ways:
+        line = jnp.concatenate(
+            [line, lax.ppermute(line, axis, [(d, (d - have) % ways) for d in range(ways)])],
+            axis=dim,
+        )
+        have = 2 * have
+    return jnp.roll(line, here * step, axis=dim)
 
 
 def shards(queries, labels, pages):
@@ -44,7 +56,7 @@
 
     empty_pages = jnp.zeros((pages_here, patch_count, width), jnp.float32)
     every_query, every_label = (
-        lax.all_gather(queries, ("dp", "inner"), axis=0, tiled=True),
+        gather_by_bits(queries, ("dp", "inner"), 0),
         lax.all_gather(labels, ("dp", "inner"), axis=0, tiled=True),
     )
     page_grads = empty_pages

time: 224 us -> 210 us (0.938)
  blocking collectives: 83.4 us -> 41.9 us
  waiting for transfers between devices: 53.7 us -> 69.7 us
  starting transfers between devices: 0.08 us -> 8.25 us
    all_gather x1 -> x0, blocking collectives: 41.4 us -> none  [shards(): lax.all_gather(queries, ('dp', 'inner'), axis=0, tiled=True)]
    ppermute x0 -> x5, waiting for transfers between devices: none -> 12.8 us  [gather_by_bits(): lax.ppermute(line, axis, [(d, (d - have) % ways) for d in range(ways)])]
    ppermute x0 -> x5, starting transfers between devices: none -> 8.17 us  [gather_by_bits(): lax.ppermute(line, axis, [(d, (d - have) % ways) for d in range(ways)])]
    reduce_scatter x1, waiting for transfers between devices: 21.7 us -> 24.9 us  [shards(): lax.psum_scatter(grad_buffer.astype(jnp.bfloat16), 'dp', scatter_dimensio...]
  transfers between devices with their start and end apart: 2 -> 7, of which waited for: 2 -> 6; matrix products, arithmetic and copies ran while one was open for 0% -> 0% of each run, Pallas kernels for 0% -> 0%
where the time goes in v1:
time: 210 us; the launch traced here: 209 us
  waiting for transfers between devices  69.7 us (33%)
  blocking collectives  41.9 us (20%)
  other arithmetic  39.3 us (19%)
  matrix products  21.1 us (10%)
  between operations  14.7 us (7%)
  local copies, waits for them, and re-layouts  13.8 us (7%)
  starting transfers between devices  8.25 us (4%)
    unnamed x1, blocking collectives  41.9 us
    reduce_scatter x1, waiting for transfers between devices, shards(): lax.psum_scatter(partial_sum, 'inner', scatter_dimension=0, tiled=True)  31.9 us
    reduce_scatter x1, waiting for transfers between devices, shards(): lax.psum_scatter(grad_buffer.astype(jnp.bfloat16), 'dp', scatter_dimensio...  24.9 us
    convert_element_type x8, other arithmetic, block_terms(): (row_grad[:, None] * weights * (1.0 + scores - matched[:, None])).astype(...  18.5 us
    ppermute x5, waiting for transfers between devices, gather_by_bits(): lax.ppermute(line, axis, [(d, (d - have) % ways) for d in range(ways)])  12.8 us
    dot_general x8, matrix products, block_terms(): jnp.dot(dscore, page_block, preferred_element_type=jnp.float32)  9.52 us
    ppermute x5, starting transfers between devices, gather_by_bits(): lax.ppermute(line, axis, [(d, (d - have) % ways) for d in range(ways)])  8.17 us
    dot_general x8, matrix products, block_terms(): lax.dot_general(dscore, flat_rows, (((0,), (0,)), ((), ())), preferred_el...  7.48 us
  transfers between devices with their start and end apart: 7, of which 6 were waited for; matrix products, arithmetic and copies ran while one was open for 0% of the time, Pallas kernels for 0%

profile of v1, /device:TPU:0, one launch (start us, length us, event | category | flops | bytes accessed | tf_op | source)
XLA Modules:
  0.0 209.2 jit_solution(15622140624398550905)
XLA Ops:
  7.2 6.5 %collective-permute-start = (bf16[1,32,128]{2,1,0:T(8,128)(2,1)}, bf16[1,32,128]{2,1,0:T(8,128)(2,1)S(1)}, u32[]{:S(2)}, u32[]{:S(2)}) collective-permute-start(bf16[1,32,128]{2,1,0:T(8,128)(2,1)} %param.5), channel_id=1, source_target_pairs={{0,31},{1,0},{2,1},{3,2},{4,3},{5,4},{6,5},{7,6},{8,7},{9,8},{10,9... | collective-permute-start | bytes 24584 | tf_op jit(solution)/shard_map/ppermute | solution.py:12
  14.4 0.8 collective-permute-done
  16.5 3.2 %collective-permute-done.1 = bf16[2,32,128]{2,1,0:T(8,128)(2,1)S(1)} collective-permute-done((bf16[2,32,128]{2,1,0:T(8,128)(2,1)S(1)}, bf16[2,32,128]{2,1,0:T(8,128)(2,1)S(1)}, u32[]{:S(2)}, u32[]{:S(2)}) %collective-permute-start.1) | collective-permute-done | bytes 16416 | tf_op jit(solution)/shard_map/ppermute | solution.py:12
  20.4 4.8 %collective-permute-done.2 = bf16[4,32,128]{2,1,0:T(8,128)(2,1)S(1)} collective-permute-done((bf16[4,32,128]{2,1,0:T(8,128)(2,1)S(1)}, bf16[4,32,128]{2,1,0:T(8,128)(2,1)S(1)}, u32[]{:S(2)}, u32[]{:S(2)}) %collective-permute-start.2) | collective-permute-done | bytes 32800 | tf_op jit(solution)/shard_map/ppermute | solution.py:12
  26.5 4.0 %collective-permute-done.3 = bf16[8,32,128]{2,1,0:T(8,128)(2,1)S(1)} collective-permute-done((bf16[8,32,128]{2,1,0:T(8,128)(2,1)S(1)}, bf16[8,32,128]{2,1,0:T(8,128)(2,1)S(1)}, u32[]{:S(2)}, u32[]{:S(2)}) %collective-permute-start.3) | collective-permute-done | bytes 65568 | tf_op jit(solution)/shard_map/ppermute | solution.py:12
  31.9 41.9 %all-reduce = s32[32]{0:T(128)S(1)} all-reduce(s32[32]{0:T(128)S(1)} %dynamic-update-slice), channel_id=1, replica_groups=mesh['dp'=4,'inner'=8] {'dp','inner'}, use_global_device_ids=true, to_apply=%add | all-reduce | flops 32 | bytes 256
  74.7 1.5 broadcast_in_dim.86
  76.2 67.8 %while.15 = (s32[]{:T(128)}, f32[4,1024,128]{2,1,0:T(8,128)}, bf16[2,16,32,128]{3,2,1,0:T(8,128)(2,1)}, s32[2,16]{1,0:T(2,128)S(1)}, s32[]{:T(128)}, /*index=5*/...) while((s32[]{:T(128)}, f32[4,1024,128]{2,1,0:T(8,128)}, ...), condition=%wide.region_17.18_spmd, body=%wide.region_0.17_spmd.sunk | while | flops 1642328576 | bytes 108293800 | solution.py:71
  77.2 0.8 copy-done
  82.7 0.8 copy-done.2
  85.1 2.3 %multiply_convert_fusion.11 = bf16[512,1024]{1,0:T(8,128)(2,1)S(1)} fusion(f32[512,1024]{1,0:T(8,128)} %copy-done.2, f32[512]{0:T(512)S(1)} %multiply_reduce_fusion.9, f32[512]{0:T(512)S(1)} %mul.312, f32[512]{0:T(512)S(1)} %fusion.117, f32[512]{0:T(512)S(1)} %get-tuple-element.258), kind=kLoop, calls=%fused_computation.10.clone.1 | loop fusion | flops 3670016 | bytes 3153920 | tf_op jit(solution)/shard_map/while/body/eval_jaxpr/convert_element_type | solution.py:45
  87.8 2.3 %fusion.125 = f32[1,1024,128]{2,1,0:T(8,128)} fusion(bf16[512,1024]{1,0:T(8,128)(2,1)S(1)} %multiply_convert_fusion.11, bf16[512,128]{1,0:T(8,128)(2,1)S(1)} %bitcast.155, f32[4,1024,128]{2,1,0:T(8,128)} %get-tuple-element.281), kind=kOutput, calls=%fused_computation.25.clone.1 | convolution fusion | flops 134348800 | bytes 2228224 | tf_op jit(solution)/shard_map/while/body/eval_jaxpr/dot_general | solution.py:51
  93.4 3.2 %multiply_convert_fusion.8 = bf16[512,1024]{1,0:T(8,128)(2,1)} fusion(f32[512,1024]{1,0:T(8,128)} %copy-done.1, f32[512]{0:T(512)S(1)} %multiply_reduce_fusion.8, f32[512]{0:T(512)S(1)} %mul.309, f32[512]{0:T(512)S(1)} %fusion.115, f32[512]{0:T(512)S(1)} %get-tuple-element.256), kind=kLoop, calls=%fused_computation.1.clone.1 | loop fusion | flops 3670016 | bytes 3153920 | tf_op jit(solution)/shard_map/while/body/eval_jaxpr/convert_element_type | solution.py:45
  96.8 2.3 %multiply_convert_fusion.9 = bf16[512,1024]{1,0:T(8,128)(2,1)S(1)} fusion(f32[512,1024]{1,0:T(8,128)} %copy-done, f32[512]{0:T(512)} %copy-done.10, f32[512]{0:T(512)S(1)} %mul.310, f32[512]{0:T(512)} %copy-done.12, f32[512]{0:T(512)S(1)} %get-tuple-element.263), kind=kLoop, calls=%fused_computation.4.clone.1 | loop fusion | flops 3670016 | bytes 3153920 | tf_op jit(solution)/shard_map/while/body/eval_jaxpr/convert_element_type | solution.py:45
  100.4 1.5 multiply_convert_fusion.10
  101.9 1.4 convolution_add_fusion.10
  103.8 1.5 convolution_add_fusion.11
  105.8 1.4 convolution_add_fusion.12
  107.8 1.6 pad_maximum_fusion.5
  111.1 0.8 copy-done
  119.0 2.3 %multiply_convert_fusion.11 = bf16[512,1024]{1,0:T(8,128)(2,1)S(1)} fusion(f32[512,1024]{1,0:T(8,128)} %copy-done.2, f32[512]{0:T(512)S(1)} %multiply_reduce_fusion.9, f32[512]{0:T(512)S(1)} %mul.312, f32[512]{0:T(512)S(1)} %fusion.117, f32[512]{0:T(512)S(1)} %get-tuple-element.258), kind=kLoop, calls=%fused_computation.10.clone.1 | loop fusion | flops 3670016 | bytes 3153920 | tf_op jit(solution)/shard_map/while/body/eval_jaxpr/convert_element_type | solution.py:45
  121.7 2.3 %fusion.125 = f32[1,1024,128]{2,1,0:T(8,128)} fusion(bf16[512,1024]{1,0:T(8,128)(2,1)S(1)} %multiply_convert_fusion.11, bf16[512,128]{1,0:T(8,128)(2,1)S(1)} %bitcast.155, f32[4,1024,128]{2,1,0:T(8,128)} %get-tuple-element.281), kind=kOutput, calls=%fused_computation.25.clone.1 | convolution fusion | flops 134348800 | bytes 2228224 | tf_op jit(solution)/shard_map/while/body/eval_jaxpr/dot_general | solution.py:51
  127.3 3.2 %multiply_convert_fusion.8 = bf16[512,1024]{1,0:T(8,128)(2,1)} fusion(f32[512,1024]{1,0:T(8,128)} %copy-done.1, f32[512]{0:T(512)S(1)} %multiply_reduce_fusion.8, f32[512]{0:T(512)S(1)} %mul.309, f32[512]{0:T(512)S(1)} %fusion.115, f32[512]{0:T(512)S(1)} %get-tuple-element.256), kind=kLoop, calls=%fused_computation.1.clone.1 | loop fusion | flops 3670016 | bytes 3153920 | tf_op jit(solution)/shard_map/while/body/eval_jaxpr/convert_element_type | solution.py:45
  130.7 2.3 %multiply_convert_fusion.9 = bf16[512,1024]{1,0:T(8,128)(2,1)S(1)} fusion(f32[512,1024]{1,0:T(8,128)} %copy-done, f32[512]{0:T(512)} %copy-done.10, f32[512]{0:T(512)S(1)} %mul.310, f32[512]{0:T(512)} %copy-done.12, f32[512]{0:T(512)S(1)} %get-tuple-element.263), kind=kLoop, calls=%fused_computation.4.clone.1 | loop fusion | flops 3670016 | bytes 3153920 | tf_op jit(solution)/shard_map/while/body/eval_jaxpr/convert_element_type | solution.py:45
  134.3 1.5 multiply_convert_fusion.10
  135.8 1.4 convolution_add_fusion.10
  137.7 1.5 convolution_add_fusion.11
  139.7 1.4 convolution_add_fusion.12
  141.7 1.6 pad_maximum_fusion.5
  144.0 24.9 %reduce-scatter.3.cloned.1.call-done = bf16[8,32,128]{2,1,0:T(8,128)(2,1)} async-done(((bf16[32,32,128]{2,1,0:T(8,128)(2,1)}), bf16[8,32,128]{2,1,0:T(8,128)(2,1)}) %reduce-scatter.3.cloned.1.call-update) | async-done | bytes 65552 | tf_op jit(solution)/shard_map/reduce_scatter | solution.py:73
  169.0 1.5 convert_element_type.39
  170.5 31.9 %reduce-scatter.5.cloned.1.call-done = f32[1,32,128]{2,1,0:T(8,128)} async-done(((f32[8,32,128]{2,1,0:T(8,128)}), f32[1,32,128]{2,1,0:T(8,128)}) %reduce-scatter.5.cloned.1.call-update) | async-done | bytes 16400 | tf_op jit(solution)/shard_map/reduce_scatter | solution.py:76
  (176 shorter events, 35.6 us)
Async XLA Ops:
  7.2 69.0 %copy-start.4 = (bf16[4,1024,128]{2,1,0:T(8,128)(2,1)S(1)}, bf16[4,1024,128]{2,1,0:T(8,128)(2,1)}, u32[]{:S(2)}) copy-start(bf16[4,1024,128]{2,1,0:T(8,128)(2,1)} %param.7) | copy-start | bytes 3145732
  7.2 161.8 %reduce-scatter.3.cloned.1.call-start = ((), (), s32[]{:S(2)}) async-start(), calls=%async_computation.2 | async-start | bytes 327680 | tf_op jit(solution)/shard_map/reduce_scatter | solution.py:73
  7.2 8.0 %collective-permute-start = (bf16[1,32,128]{2,1,0:T(8,128)(2,1)}, bf16[1,32,128]{2,1,0:T(8,128)(2,1)S(1)}, u32[]{:S(2)}, u32[]{:S(2)}) collective-permute-start(bf16[1,32,128]{2,1,0:T(8,128)(2,1)} %param.5), channel_id=1, source_target_pairs={{0,31},{1,0},{2,1},{3,2},{4,3},{5,4},{6,5},{7,6},{8,7},{9,8},{10,9... | collective-permute-start | bytes 24584 | tf_op jit(solution)/shard_map/ppermute | solution.py:12
  16.0 3.7 %collective-permute-start.1 = (bf16[2,32,128]{2,1,0:T(8,128)(2,1)S(1)}, bf16[2,32,128]{2,1,0:T(8,128)(2,1)S(1)}, u32[]{:S(2)}, u32[]{:S(2)}) collective-permute-start(bf16[2,32,128]{2,1,0:T(8,128)(2,1)S(1)} %pad_maximum_fusion.3), channel_id=1, source_target_pairs={{0,30},{1,31},{2,0},{3,1},{4,2},{5,3},{6,4},{7,5},{8,6},{9,7},{10,... | collective-permute-start | bytes 49160 | tf_op jit(solution)/shard_map/ppermute | solution.py:12
  20.4 4.8 %collective-permute-start.2 = (bf16[4,32,128]{2,1,0:T(8,128)(2,1)S(1)}, bf16[4,32,128]{2,1,0:T(8,128)(2,1)S(1)}, u32[]{:S(2)}, u32[]{:S(2)}) collective-permute-start(bf16[4,32,128]{2,1,0:T(8,128)(2,1)S(1)} %pad_maximum_fusion.2), channel_id=1, source_target_pairs={{0,28},{1,29},{2,30},{3,31},{4,0},{5,1},{6,2},{7,3},{8,4},{9,5},{1... | collective-permute-start | bytes 98312 | tf_op jit(solution)/shard_map/ppermute | solution.py:12
  25.9 4.6 %collective-permute-start.3 = (bf16[8,32,128]{2,1,0:T(8,128)(2,1)S(1)}, bf16[8,32,128]{2,1,0:T(8,128)(2,1)S(1)}, u32[]{:S(2)}, u32[]{:S(2)}) collective-permute-start(bf16[8,32,128]{2,1,0:T(8,128)(2,1)S(1)} %pad_maximum_fusion.1), channel_id=1, source_target_pairs={{0,24},{1,25},{2,26},{3,27},{4,28},{5,29},{6,30},{7,31},{8,0},{9,1... | collective-permute-start | bytes 196616 | tf_op jit(solution)/shard_map/ppermute | solution.py:12
  30.5 43.4 %collective-permute-start.4 = (bf16[16,32,128]{2,1,0:T(8,128)(2,1)S(1)}, bf16[16,32,128]{2,1,0:T(8,128)(2,1)S(1)}, u32[]{:S(2)}, u32[]{:S(2)}) collective-permute-start(bf16[16,32,128]{2,1,0:T(8,128)(2,1)S(1)} %get-tuple-element.171), channel_id=1, source_target_pairs={{0,16},{1,17},{2,18},{3,19},{4,20},{5,21},{6,22},{7,23},{8,24},{9,... | collective-permute-start | bytes 393224 | tf_op jit(solution)/shard_map/ppermute | solution.py:12
  76.2 8.2 %copy-start.18 = (s32[2,16]{1,0:T(2,128)}, s32[2,16]{1,0:T(2,128)S(1)}, u32[]{:S(2)}) copy-start(s32[2,16]{1,0:T(2,128)S(1)} %get-tuple-element.295) | copy-start | bytes 388 | tf_op jit(solution)/shard_map/while
  78.1 1.8 copy-start.12
  78.7 1.7 copy-start.10
  90.6 2.1 copy-start.15
  90.7 2.1 copy-start.16
  90.7 2.1 copy-start.17
  100.4 2.9 %copy-start.6 = (f32[4,1024,128]{2,1,0:T(8,128)S(1)}, f32[4,1024,128]{2,1,0:T(8,128)}, u32[]{:S(2)}) copy-start(f32[4,1024,128]{2,1,0:T(8,128)} %get-tuple-element.281) | copy-start | bytes 6291460 | tf_op jit(solution)/shard_map/while
  103.8 2.0 copy-start.3
  105.8 1.9 copy-start.7
  107.7 2.3 %copy-start.5 = (bf16[4,1024,128]{2,1,0:T(8,128)(2,1)S(1)}, bf16[4,1024,128]{2,1,0:T(8,128)(2,1)}, u32[]{:S(2)}) copy-start(bf16[4,1024,128]{2,1,0:T(8,128)(2,1)} %get-tuple-element.318) | copy-start | bytes 3145732 | tf_op jit(solution)/shard_map/while
  107.7 2.3 %copy-start.9 = (bf16[2,16,32,128]{3,2,1,0:T(8,128)(2,1)S(1)}, bf16[2,16,32,128]{3,2,1,0:T(8,128)(2,1)}, u32[]{:S(2)}) copy-start(bf16[2,16,32,128]{3,2,1,0:T(8,128)(2,1)} %copy-done.8) | copy-start | bytes 786436 | tf_op jit(solution)/shard_map/while
  107.7 2.3 %copy-start.19 = (s32[2,16]{1,0:T(2,128)S(1)}, s32[2,16]{1,0:T(2,128)}, u32[]{:S(2)}) copy-start(s32[2,16]{1,0:T(2,128)} %copy-done.18) | copy-start | bytes 388 | tf_op jit(solution)/shard_map/while
  110.1 8.2 %copy-start.18 = (s32[2,16]{1,0:T(2,128)}, s32[2,16]{1,0:T(2,128)S(1)}, u32[]{:S(2)}) copy-start(s32[2,16]{1,0:T(2,128)S(1)} %get-tuple-element.295) | copy-start | bytes 388 | tf_op jit(solution)/shard_map/while
  112.0 1.8 copy-start.12
  112.6 1.7 copy-start.10
  124.6 2.1 copy-start.15
  124.6 2.1 copy-start.16
  124.6 2.1 copy-start.17
  134.3 2.9 %copy-start.6 = (f32[4,1024,128]{2,1,0:T(8,128)S(1)}, f32[4,1024,128]{2,1,0:T(8,128)}, u32[]{:S(2)}) copy-start(f32[4,1024,128]{2,1,0:T(8,128)} %get-tuple-element.281) | copy-start | bytes 6291460 | tf_op jit(solution)/shard_map/while
  137.7 2.0 copy-start.3
  139.7 1.9 copy-start.7
  141.6 2.3 %copy-start.5 = (bf16[4,1024,128]{2,1,0:T(8,128)(2,1)S(1)}, bf16[4,1024,128]{2,1,0:T(8,128)(2,1)}, u32[]{:S(2)}) copy-start(bf16[4,1024,128]{2,1,0:T(8,128)(2,1)} %get-tuple-element.318) | copy-start | bytes 3145732 | tf_op jit(solution)/shard_map/while
  141.6 2.3 %copy-start.9 = (bf16[2,16,32,128]{3,2,1,0:T(8,128)(2,1)S(1)}, bf16[2,16,32,128]{3,2,1,0:T(8,128)(2,1)}, u32[]{:S(2)}) copy-start(bf16[2,16,32,128]{3,2,1,0:T(8,128)(2,1)} %copy-done.8) | copy-start | bytes 786436 | tf_op jit(solution)/shard_map/while
  141.7 2.3 %copy-start.19 = (s32[2,16]{1,0:T(2,128)S(1)}, s32[2,16]{1,0:T(2,128)}, u32[]{:S(2)}) copy-start(s32[2,16]{1,0:T(2,128)} %copy-done.18) | copy-start | bytes 388 | tf_op jit(solution)/shard_map/while
  144.0 58.4 %reduce-scatter.5.cloned.1.call-start = ((), (), s32[]{:S(2)}) async-start(), calls=%async_computation.3 | async-start | bytes 147456 | tf_op jit(solution)/shard_map/reduce_scatter | solution.py:76
  (14 other events, 16.0 us)
Sparse Core Ops, SparseCore 0:
  144.1 24.7 reduce-scatter.2
  171.8 30.5 reduce-scatter.4
